TPU v7x, 32 devices: a whole 2x2x4 slice. The times are simulated.
32 devices in a mesh: cables: 2 (over x), chan: 16 (over z, y, core).
Axes of the slice: x: 2, y: 2, z: 4, core: 2. Of those that a mesh axis runs over, the one named last changes fastest.
Arguments:
- traces: bfloat16 [4096, 128], P(('cables', 'chan')), parts along dimension 0, may hold values from -30 to 30
- filter_coefs: float32 [16, 5], replicated, may hold values from -2 to 2, as said below
- leakage: bfloat16 [4096, 16], P(('cables', 'chan')), parts along dimension 0, may hold values from 0 to 1
- live_mask: int32 [4096], P(('cables', 'chan')), parts along dimension 0, may hold values 0 or 1
- aperture_starts: int32 [32], P(('cables', 'chan')), parts along dimension 0, may hold values from 0 to 2047, as said below
- delays: int32 [256, 512], replicated, may hold values from 0 to 15
- refine_lists: int32 [32, 2, 8], P(('cables', 'chan')), parts along dimension 0, may hold values from 0 to 255
Outputs:
- beam_power: bfloat16 [32, 256, 16, 128], P(('cables', 'chan')), parts along dimension 0
- refined_power: bfloat16 [32, 2, 8, 16, 128], P(('cables', 'chan')), parts along dimension 0
There are 2 independent parts, one for each index of `cables`. A program takes and returns all parts, laid end to end along the dimension named above; an argument that names none is the same for every part. Nothing has to cross between parts.
Inputs may be any that keep to these rules, and one draw needn't show every extreme that they name: `aperture_starts`: aperture a begins at one of the 128 channels of block a // 1 of the cable (channels (a) * 128 up to that plus 128 - 1). `filter_coefs`: each band is a stable bandpass biquad.
All inputs are finite; a program needn't handle non-finite values. No bound on the sum of `live_mask` on one device may be relied on, other than what follows from the above.
Results may differ from a plain program's by a relative error of at most 0.0065.
Values may be sent and summed in bfloat16 or wider, within the bound.
A program may use at most 192 MiB of HBM per device.

v0:
```python
import math

import jax
import jax.numpy as jnp
from jax import lax
from jax.sharding import PartitionSpec as P

DMAX = 16
BLK = 64


eps_norm = 1e-06


def prefix(part, axis, combine, identity):
    place = lax.axis_index(axis)
    gathered = jax.tree.map(lambda a: lax.all_gather(a, axis), part)
    state = jax.tree.map(lambda a, e: jnp.zeros_like(a) + jnp.asarray(e, a.dtype), part, identity)

    def one(lap, state):
        return combine(
            state, jax.tree.map(lambda a: lax.dynamic_index_in_dim(a, lap, 0, False), gathered)
        )

    return lax.fori_loop(0, place, one, state)


def passed_along(block, axis, distance):
    devices = range(lax.axis_size(axis))
    route = [(i - distance, i) for i in devices if i - distance in devices]
    return lax.ppermute(block, axis, route)


def trend_combine(earlier, later):
    return (earlier[0] * later[0], later[0] * earlier[1] + later[1])


def hilbert_table(samples):
    indices = jnp.arange(samples)
    offset = (indices[None, :] - indices[:, None]) % samples
    is_odd = offset % 2 == 1
    phases = jnp.pi * offset.astype(jnp.float32) / samples
    divisor = jnp.where(is_odd, jnp.sin(phases), 1.0)
    return jnp.where(is_odd, 2.0 / samples * jnp.cos(phases) / divisor, 0.0)


def envelope_power(signal, hilbert):
    turned = jnp.dot(
        signal, hilbert, precision=lax.Precision.HIGHEST, preferred_element_type=jnp.float32
    )
    return (signal * signal + turned * turned).astype(jnp.bfloat16)


def response_table(coefficients, block_len):
    table_width = block_len + 4
    positions = jnp.arange(table_width)
    band_count = coefficients.shape[0]
    b_zero = coefficients[:, 0:1]
    b_one = coefficients[:, 1:2]
    b_two = coefficients[:, 2:3]
    a_one = coefficients[:, 3:4]
    a_two = coefficients[:, 4:5]

    def unit_vector(place):
        return jnp.broadcast_to(
            (positions == place).astype(jnp.float32)[None], (band_count, table_width)
        )

    def advance(carry_state, moment):
        in_last, in_before, out_last, out_before = carry_state
        in_now = unit_vector(moment)
        out_now = (
            b_zero * in_now
            + b_one * in_last
            + b_two * in_before
            - a_one * out_last
            - a_two * out_before
        )
        return ((in_now, in_last, out_now, out_last), out_now)

    initial = (
        unit_vector(block_len + 1),
        unit_vector(block_len),
        unit_vector(block_len + 3),
        unit_vector(block_len + 2),
    )
    _, outputs = lax.scan(advance, initial, jnp.arange(block_len))
    return jnp.transpose(outputs, (1, 2, 0))


def filter_bank(raw_traces, coefficients):
    chan_count, samples = raw_traces.shape
    band_count = coefficients.shape[0]
    block_len = BLK
    blocks = samples // block_len
    kernel = response_table(coefficients, block_len)
    signal = raw_traces.astype(jnp.float32).reshape(chan_count, blocks, block_len)
    before = jnp.concatenate(
        [jnp.zeros((chan_count, 1, 2), jnp.float32), signal[:, :-1, block_len - 2 :]], axis=1
    )
    inputs = jnp.concatenate([signal, before], axis=2)
    forced = jnp.einsum(
        "cmi,bij->mcbj", inputs, kernel[:, : block_len + 2], precision=lax.Precision.HIGHEST
    )
    tail_two = kernel[:, block_len + 2][None]
    tail_one = kernel[:, block_len + 3][None]

    def carry_block(carry_state, block_now):
        out_before, out_last = carry_state
        block_now = block_now + out_before[..., None] * tail_two + out_last[..., None] * tail_one
        return ((block_now[..., block_len - 2], block_now[..., block_len - 1]), block_now)

    zero_state = jnp.zeros((chan_count, band_count), jnp.float32)
    _, outputs = lax.scan(carry_block, (zero_state, zero_state), forced)
    return jnp.transpose(outputs, (1, 2, 0, 3)).reshape(chan_count, band_count, samples)


def local_trend(filtered, leakage):
    leak_rate = leakage.astype(jnp.float32)
    retention = jnp.exp(-leak_rate)[..., None]
    inflow = -jnp.expm1(-leak_rate)[..., None]
    return lax.associative_scan(
        trend_combine, (retention, inflow * filtered.astype(jnp.float32)), axis=0
    )


def carried(keep_last, trend_last):
    identity = (jnp.ones_like(keep_last), jnp.zeros_like(trend_last))
    return prefix((keep_last, trend_last), "chan", trend_combine, identity)[1]


def delayed_copies(window, samples):
    lag_ids = jnp.arange(DMAX)[:, None, None]
    source = jnp.arange(samples)[None, :, None]
    target = jnp.arange(samples)[None, None, :]
    move_table = (target - source == lag_ids).astype(jnp.bfloat16)
    return jnp.einsum("kbs,dst->dkbt", window, move_table, preferred_element_type=jnp.bfloat16)


def shifted_window(copies, delay_now):
    section = lax.dynamic_index_in_dim(copies, delay_now, 0, keepdims=False)
    return section.reshape(section.shape[0], -1)


def slant_stack(copies, delays):
    summed = jnp.zeros((delays.shape[0], copies.shape[2] * copies.shape[3]), jnp.float32)

    def add_delay(delay_now, running):
        picked = (delays == delay_now).astype(jnp.bfloat16)
        return running + jnp.dot(
            picked, shifted_window(copies, delay_now), preferred_element_type=jnp.float32
        )

    return lax.fori_loop(0, DMAX, add_delay, summed)


def refine_pass(copies, guide_trace, chosen, live_window):
    slot_count = guide_trace.shape[0]
    aperture_len = chosen.shape[1]

    def measure(delay_now, running):
        numerator, energy = running
        window = shifted_window(copies, delay_now)
        matches = (chosen == delay_now).astype(jnp.float32)
        products = lax.dot_general(
            guide_trace, window, (((1,), (1,)), ((), ())), preferred_element_type=jnp.float32
        )
        squares = jnp.sum(jnp.square(window.astype(jnp.float32)), axis=1)
        return (numerator + matches * products, energy + matches * squares[None])

    empty_acc = jnp.zeros((slot_count, aperture_len), jnp.float32)
    numerator, energy = lax.fori_loop(0, DMAX, measure, (empty_acc, empty_acc))
    guide_f = guide_trace.astype(jnp.float32)
    guide_norm = jnp.sqrt(jnp.sum(guide_f * guide_f, axis=1) + eps_norm)
    coherence = numerator / (jnp.sqrt(energy + eps_norm) * guide_norm[:, None])
    weight = (live_window[None] * (0.25 + jnp.maximum(coherence, 0.0))).astype(jnp.bfloat16)

    def gather_delay(delay_now, running):
        picked = jnp.where(chosen == delay_now, weight, jnp.zeros_like(weight))
        return running + jnp.dot(
            picked, shifted_window(copies, delay_now), preferred_element_type=jnp.float32
        )

    summed = lax.fori_loop(
        0, DMAX, gather_delay, jnp.zeros((slot_count, guide_trace.shape[1]), jnp.float32)
    )
    weight_f = weight.astype(jnp.float32)
    return summed / jnp.sqrt(1.0 + jnp.sum(weight_f * weight_f, axis=1))[:, None]


def per_device(traces, filter_coefs, leakage, live_mask, aperture_starts, delays, refine_lists):
    chan_count, samples = traces.shape
    band_count = filter_coefs.shape[0]
    slowness_count = delays.shape[0]
    aperture_len = delays.shape[1]
    neighbours = (aperture_len + chan_count - 1) // chan_count
    live_flag = live_mask.astype(jnp.float32)
    live_small = live_mask.astype(jnp.bfloat16)
    filtered = (live_flag[:, None, None] * filter_bank(traces, filter_coefs)).astype(jnp.bfloat16)
    retention, running_mean = local_trend(filtered, leakage)
    incoming = carried(retention[chan_count - 1], running_mean[chan_count - 1])
    detrended = (
        live_flag[:, None, None]
        * (filtered.astype(jnp.float32) - (running_mean + retention * incoming[None]))
    ).astype(jnp.bfloat16)
    detr_parts = [detrended]
    live_parts = [live_small]
    for offset in range(1, neighbours + 1):
        received = passed_along((detrended, live_small), "chan", -offset)
        detr_parts.append(received[0])
        live_parts.append(received[1])
    extended = jnp.concatenate(detr_parts, axis=0)
    wide_live = jnp.concatenate(live_parts, axis=0).astype(jnp.float32)
    hilbert = hilbert_table(samples)
    first_chan = lax.axis_index("chan") * chan_count
    slowness_ids = jnp.arange(slowness_count)
    offset_in = aperture_starts[0] - first_chan
    window = lax.dynamic_slice_in_dim(extended, offset_in, aperture_len, 0)
    live_window = lax.dynamic_slice_in_dim(wide_live, offset_in, aperture_len, 0)
    copies = delayed_copies(window, samples)
    stacked = slant_stack(copies, delays) * (1.0 / math.sqrt(aperture_len))
    beam_list = [
        envelope_power(stacked.reshape(-1, samples), hilbert).reshape(
            slowness_count, band_count, samples
        )
    ]
    guide_trace = stacked
    passes = []
    for pass_index in range(refine_lists.shape[1]):
        picked_rows = (refine_lists[0, pass_index][:, None] == slowness_ids[None]).astype(
            jnp.float32
        )
        chosen = jnp.dot(
            picked_rows, delays.astype(jnp.float32), precision=lax.Precision.HIGHEST
        ).astype(jnp.int32)
        if pass_index == 0:
            guide_trace = jnp.dot(picked_rows, stacked, precision=lax.Precision.HIGHEST)
        refined = refine_pass(copies, guide_trace.astype(jnp.bfloat16), chosen, live_window)
        passes.append(
            envelope_power(refined.reshape(-1, samples), hilbert).reshape(-1, band_count, samples)
        )
        guide_trace = refined
    refined_list = [jnp.stack(passes)]
    return (jnp.stack(beam_list), jnp.stack(refined_list))


def solution(mesh):
    return jax.shard_map(
        per_device,
        mesh=mesh,
        in_specs=(
            P(("cables", "chan"), None),
            P(),
            P(("cables", "chan"), None),
            P(("cables", "chan")),
            P(("cables", "chan")),
            P(),
            P(("cables", "chan"), None, None),
        ),
        out_specs=(
            P(("cables", "chan"), None, None, None),
            P(("cables", "chan"), None, None, None, None),
        ),
        check_vma=False,
    )
```

profile of v0, /device:TPU:0, one launch (start us, length us, event | category | flops | bytes accessed | tf_op | source)
XLA Modules:
  0.0 596.6 jit_solution(10434142678364811344)
XLA Ops:
  1.6 99.2 %while.121 = (s32[]{:T(128)}, f32[16,68]{1,0:T(8,128)S(1)}, f32[16,68]{1,0:T(8,128)S(1)}, f32[16,68]{1,0:T(8,128)S(1)}, f32[16,68]{1,0:T(8,128)S(1)}, /*index=5*...) while((s32[]{:T(128)}, f32[16,68]{1,0:T(8,128)S(1)}, ...), condition=%wide.region_1.2_spmd.clone, body=%wide.region_0.1_spmd.clone.sunk | while | flops 9930 | bytes 62217 | solution.py:87
  124.5 6.2 %pad.100 = f32[128,16,128]{2,0,1:T(8,128)S(1)} pad(f32[64,16,128]{2,0,1:T(8,128)} %add.424, f32[]{:T(128)} %constant.232.clone.1), padding=1_0_1x0_0_0x0_0_0 | pad | bytes 1572868 | tf_op jit(solution)/shard_map/pad | solution.py:122
  130.7 23.5 %all_gather.7 = f32[16,16,128]{2,1,0:T(8,128)S(1)} all-gather(f32[1,16,128]{2,1,0:T(8,128)S(1)} %bitcast.239), channel_id=1, replica_groups=mesh['cables'=2,'chan'=16] {'chan'}, dimensions={0}, use_global_device_ids=true | all-gather | bytes 139264 | tf_op jit(solution)/shard_map/all_gather | solution.py:17
  154.3 17.4 %all_gather.6 = f32[16,16,1]{1,2,0:T(1,128)S(1)} all-gather(f32[1,16,1]{1,2,0:T(1,128)S(1)} %copy.211), channel_id=1, replica_groups=mesh['cables'=2,'chan'=16] {'chan'}, dimensions={0}, use_global_device_ids=true | all-gather | bytes 1088 | tf_op jit(solution)/shard_map/all_gather | solution.py:17
  185.1 18.6 %collective-permute-done.5 = bf16[128]{0:T(256)(128)(2,1)S(1)} collective-permute-done((bf16[128]{0:T(256)(128)(2,1)S(1)}, bf16[128]{0:T(256)(128)(2,1)S(1)}, u32[]{:S(2)}, u32[]{:S(2)}) %collective-permute-start.5) | collective-permute-done | bytes 288 | tf_op jit(solution)/shard_map/ppermute | solution.py:31
  205.3 24.3 %collective-permute-done.6 = bf16[128]{0:T(256)(128)(2,1)S(1)} collective-permute-done((bf16[128]{0:T(256)(128)(2,1)S(1)}, bf16[128]{0:T(256)(128)(2,1)S(1)}, u32[]{:S(2)}, u32[]{:S(2)}) %collective-permute-start.6) | collective-permute-done | bytes 288 | tf_op jit(solution)/shard_map/ppermute | solution.py:31
  231.7 3.4 collective-permute-done.7
  240.2 15.3 %convolution_bitcast_fusion = bf16[16,512,16,128]{1,3,2,0:T(8,128)(2,1)} fusion(bf16[640,16,128]{2,0,1:T(8,128)(2,1)} %constant_dynamic-update-slice_fusion, s32[]{:T(128)S(6)} %select_n.86, s32[128,128]{0,1:T(8,128)S(1)} %iota_subtract_fusion), kind=kOutput, calls=%fused_computation.52 | convolution fusion | flops 4295229440 | bytes 35717124 | tf_op jit(solution)/shard_map/kbs,dst->dkbt/dot_general | solution.py:137
  255.5 48.9 %copy.213 = bf16[16,512,16,128]{3,2,1,0:T(8,128)(2,1)} copy(bf16[16,512,16,128]{1,3,2,0:T(8,128)(2,1)} %convolution_bitcast_fusion) | data formatting | bytes 67108864
  304.4 89.6 %while.122 = (s32[]{:T(128)}, f32[256,2048]{1,0:T(8,128)}, s32[256,512]{1,0:T(8,128)S(1)}, bf16[16,512,16,128]{3,2,1,0:T(8,128)(2,1)}, s32[]{:T(128)}, /*index=5*/s32[]{:T(128)}) while((s32[]{:T(128)}, f32[256,2048]{1,0:T(8,128)}, s32[256,512]{1,0:T(8,128)S(1)}, bf16[16,512,16,128]{3,2,1,0:T(8,128)(2,1)}, s32[]{:T(128)}, ...), condition=%wide.region_7.8_spmd.clone, body=%wide.region_6.7_spmd.clone.sunk | while | flops 538050560 | bytes 11010135 | solution.py:154
  310.5 3.7 convolution_add_fusion.6
  316.2 3.7 convolution_add_fusion.6
  321.9 3.7 convolution_add_fusion.6
  327.6 3.7 convolution_add_fusion.6
  333.3 3.7 convolution_add_fusion.6
  339.0 3.7 convolution_add_fusion.6
  344.7 3.7 convolution_add_fusion.6
  350.4 3.7 convolution_add_fusion.6
  356.1 3.7 convolution_add_fusion.6
  361.8 3.7 convolution_add_fusion.6
  367.5 3.7 convolution_add_fusion.6
  373.2 3.7 convolution_add_fusion.6
  378.9 3.7 convolution_add_fusion.6
  384.6 3.7 convolution_add_fusion.6
  390.3 3.7 convolution_add_fusion.6
  398.2 56.5 %while.123 = (s32[]{:T(128)}, f32[8,512]{1,0:T(8,128)S(1)}, f32[8,512]{1,0:T(8,128)S(1)}, s32[8,512]{1,0:T(8,128)S(1)}, bf16[16,512,16,128]{3,2,1,0:T(8,128)(2,1...) while((s32[]{:T(128)}, f32[8,512]{1,0:T(8,128)S(1)}, f32[8,512]{1,0:T(8,128)S(1)}, ...), condition=%wide.region_10.11_spmd.clone, body=%wide.region_8.10_spmd.clone.sunk | while | flops 19951108 | bytes 6418536 | solution.py:172
  405.3 2.9 multiply_reduce_fusion.8
  408.8 2.9 multiply_reduce_fusion.8
  454.9 37.8 %while.124 = (s32[]{:T(128)}, f32[8,2048]{1,0:T(8,128)S(1)}, s32[8,512]{1,0:T(8,128)S(1)}, bf16[8,512]{1,0:T(8,128)(2,1)S(1)}, bf16[16,512,16,128]{3,2,1,0:T(8,128)(2,1)}, /*index=5*/s32[]{:T(128)}, s32[]{:T(128)}) while((s32[]{:T(128)}, f32[8,2048]{1,0:T(8,128)S(1)}, s32[8,512]{1,0:T(8,128)S(1)}, ...), condition=%wide.region_13.14_spmd.clone, body=%wide.region_12.13_spmd.clone.sunk | while | flops 16818180 | bytes 6447199 | solution.py:184
  492.9 56.5 %while.125 = (s32[]{:T(128)}, f32[8,512]{1,0:T(8,128)S(1)}, f32[8,512]{1,0:T(8,128)S(1)}, s32[8,512]{1,0:T(8,128)S(1)}, bf16[16,512,16,128]{3,2,1,0:T(8,128)(2,1...) while((s32[]{:T(128)}, f32[8,512]{1,0:T(8,128)S(1)}, f32[8,512]{1,0:T(8,128)S(1)}, ...), condition=%wide.region_17.18_spmd.clone, body=%wide.region_15.17_spmd.clone.sunk | while | flops 19951108 | bytes 6418536 | solution.py:172
  549.6 37.9 %while.126 = (s32[]{:T(128)}, f32[8,2048]{1,0:T(8,128)S(1)}, s32[8,512]{1,0:T(8,128)S(1)}, bf16[8,512]{1,0:T(8,128)(2,1)S(1)}, bf16[16,512,16,128]{3,2,1,0:T(8,128)(2,1)}, /*index=5*/s32[]{:T(128)}, s32[]{:T(128)}) while((s32[]{:T(128)}, f32[8,2048]{1,0:T(8,128)S(1)}, s32[8,512]{1,0:T(8,128)S(1)}, ...), condition=%wide.region_20.21_spmd.clone, body=%wide.region_19.20_spmd.clone.sunk | while | flops 16818180 | bytes 6447199 | solution.py:184
  590.7 5.3 fusion.43
  (913 shorter events, 365.8 us)
Async XLA Ops:
  104.8 0.7 copy-start.7
  104.8 1.3 copy-start.12
  106.7 2.0 copy-start.8
  115.8 5.7 copy-start.6
  115.8 6.2 %copy-start.5 = (f32[1,16,128]{2,0,1:T(1,128)S(1)}, f32[1,16,128]{2,0,1:T(1,128)}, u32[]{:S(2)}) copy-start(f32[1,16,128]{2,0,1:T(1,128)} %slice.335) | copy-start | bytes 24580
  116.3 5.9 copy-start.4
  124.3 47.5 %copy-start.9 = (f32[128]{0:T(128)S(1)}, f32[128]{0:T(128)}, u32[]{:S(2)}) copy-start(f32[128]{0:T(128)} %copy-done.8) | copy-start | bytes 1540
  130.7 41.0 %copy-start.3 = (f32[128,16,128]{2,0,1:T(8,128)}, f32[128,16,128]{2,0,1:T(8,128)S(1)}, u32[]{:S(2)}) copy-start(f32[128,16,128]{2,0,1:T(8,128)S(1)} %pad.100) | copy-start | bytes 3145732
  171.7 7.8 %copy-start.11 = (bf16[128]{0:T(256)(128)(2,1)S(1)}, bf16[128]{0:T(256)(128)(2,1)}, u32[]{:S(2)}) copy-start(bf16[128]{0:T(256)(128)(2,1)} %get-tuple-element.1181) | copy-start | bytes 772
  171.7 9.1 %copy-start.10 = (s32[1,2,8]{2,1,0:T(2,128)S(1)}, s32[1,2,8]{2,1,0:T(2,128)}, u32[]{:S(2)}) copy-start(s32[1,2,8]{2,1,0:T(2,128)} %param.29) | copy-start | bytes 196
  171.8 9.1 %copy-start.1 = (s32[256,512]{1,0:T(8,128)S(1)}, s32[256,512]{1,0:T(8,128)}, u32[]{:S(2)}) copy-start(s32[256,512]{1,0:T(8,128)} %param.28) | copy-start | bytes 1572868
  174.3 61.0 %collective-permute-start = (bf16[128,16,128]{2,0,1:T(8,128)(2,1)S(1)}, bf16[128,16,128]{2,0,1:T(8,128)(2,1)}, u32[]{:S(2)}, u32[]{:S(2)}) collective-permute-start(bf16[128,16,128]{2,0,1:T(8,128)(2,1)S(1)} %get-tuple-element.1158), channel_id=1, source_target_pairs={{1,0},{2,1},{3,2},{4,3},{5,4},{6,5},{7,6},{8,7},{9,8},{10,9},{11,1... | collective-permute-start | bytes 1572872 | tf_op jit(solution)/shard_map/ppermute | solution.py:31
  175.6 61.7 %collective-permute-start.1 = (bf16[128,16,128]{2,0,1:T(8,128)(2,1)S(1)}, bf16[128,16,128]{2,0,1:T(8,128)(2,1)S(1)}, u32[]{:S(2)}, u32[]{:S(2)}) collective-permute-start(bf16[128,16,128]{2,0,1:T(8,128)(2,1)S(1)} %get-tuple-element.1158), channel_id=1, source_target_pairs={{2,0},{3,1},{4,2},{5,3},{6,4},{7,5},{8,6},{9,7},{10,8},{11,9},{12,... | collective-permute-start | bytes 1572872 | tf_op jit(solution)/shard_map/ppermute | solution.py:31
  176.9 61.4 %collective-permute-start.2 = (bf16[128,16,128]{2,0,1:T(8,128)(2,1)S(1)}, bf16[128,16,128]{2,0,1:T(8,128)(2,1)S(1)}, u32[]{:S(2)}, u32[]{:S(2)}) collective-permute-start(bf16[128,16,128]{2,0,1:T(8,128)(2,1)S(1)} %get-tuple-element.1158), channel_id=1, source_target_pairs={{3,0},{4,1},{5,2},{6,3},{7,4},{8,5},{9,6},{10,7},{11,8},{12,9},{13... | collective-permute-start | bytes 1572872 | tf_op jit(solution)/shard_map/ppermute | solution.py:31
  178.2 61.1 %collective-permute-start.3 = (bf16[128,16,128]{2,0,1:T(8,128)(2,1)S(1)}, bf16[128,16,128]{2,0,1:T(8,128)(2,1)S(1)}, u32[]{:S(2)}, u32[]{:S(2)}) collective-permute-start(bf16[128,16,128]{2,0,1:T(8,128)(2,1)S(1)} %get-tuple-element.1158), channel_id=1, source_target_pairs={{4,0},{5,1},{6,2},{7,3},{8,4},{9,5},{10,6},{11,7},{12,8},{13,9},{1... | collective-permute-start | bytes 1572872 | tf_op jit(solution)/shard_map/ppermute | solution.py:31
  179.5 3.7 collective-permute-start.4
  183.2 20.6 %collective-permute-start.5 = (bf16[128]{0:T(256)(128)(2,1)S(1)}, bf16[128]{0:T(256)(128)(2,1)S(1)}, u32[]{:S(2)}, u32[]{:S(2)}) collective-permute-start(bf16[128]{0:T(256)(128)(2,1)S(1)} %copy-done.11), channel_id=1, source_target_pairs={{2,0},{3,1},{4,2},{5,3},{6,4},{7,5},{8,6},{9,7},{10,8},{11,9},{12,... | collective-permute-start | bytes 776 | tf_op jit(solution)/shard_map/ppermute | solution.py:31
  203.8 25.9 %collective-permute-start.6 = (bf16[128]{0:T(256)(128)(2,1)S(1)}, bf16[128]{0:T(256)(128)(2,1)S(1)}, u32[]{:S(2)}, u32[]{:S(2)}) collective-permute-start(bf16[128]{0:T(256)(128)(2,1)S(1)} %copy-done.11), channel_id=1, source_target_pairs={{3,0},{4,1},{5,2},{6,3},{7,4},{8,5},{9,6},{10,7},{11,8},{12,9},{13... | collective-permute-start | bytes 776 | tf_op jit(solution)/shard_map/ppermute | solution.py:31
  229.6 5.5 collective-permute-start.7
  394.1 2.7 copy-start
  587.6 1.6 copy-start.2
where the time goes:
time: 603 us; the launch traced here: 597 us
  local copies, waits for them, and re-layouts  217 us (36%)
  other arithmetic  154 us (26%)
  matrix products  118 us (20%)
  waiting for transfers between devices  48 us (8%)
  blocking collectives  40.9 us (7%)
  starting transfers between devices  10.5 us (2%)
    dynamic_slice x48, local copies, waits for them, and re-layouts, shifted_window(): section = lax.dynamic_index_in_dim(copies, delay_now, 0, keepdims=False)  93.7 us
    reduce_sum x32, other arithmetic, measure(): squares = jnp.sum(jnp.square(window.astype(jnp.float32)), axis=1)  91.2 us
    dot_general x16, matrix products, add_delay(): jnp.dot(picked, shifted_window(copies, delay_now), preferred_element_type...  58.3 us
    unnamed x34, local copies, waits for them, and re-layouts  54.4 us
    ppermute x8, waiting for transfers between devices, passed_along(): return lax.ppermute(block, axis, route)  48 us
    convert_element_type x68, other arithmetic, unit_vector(): (positions == place).astype(jnp.float32)[None]  44 us
    dynamic_slice x64, local copies, waits for them, and re-layouts, response_table(): _, outputs = lax.scan(advance, initial, jnp.arange(block_len))  42.5 us
    all_gather x2, blocking collectives, prefix(): gathered = jax.tree.map(lambda a: lax.all_gather(a, axis), part)  40.9 us
  transfers between devices with their start and end apart: 8, of which 4 were waited for; matrix products, arithmetic and copies ran while one was open for 1% of the time, Pallas kernels for 0%

commit v1 on v0

v1 whole, which is shorter than its diff:
```python
import functools
import math

import numpy as np

import jax
import jax.numpy as jnp
from jax import lax
from jax.experimental import pallas as pl
from jax.experimental.pallas import tpu as pltpu
from jax.sharding import PartitionSpec as P

DMAX = 16
LANES = 128
EPS = 1e-06
MESH = pl.DeviceIdType.MESH
VM = pl.BlockSpec(memory_space=pltpu.VMEM)
SM = pl.BlockSpec(memory_space=pltpu.SMEM)
HB = pl.BlockSpec(memory_space=pl.ANY)


def hilbert_parts(samples):
    index = np.arange(samples)
    offset = (index[:, None] - index[None, :]) % samples
    odd = offset % 2 == 1
    phase = np.pi * offset / samples
    table = np.where(odd, 2.0 / samples * np.cos(phase) / np.where(odd, np.sin(phase), 1.0), 0.0)
    table = table.astype(np.float32)
    high = table.astype(jnp.bfloat16)
    low = (table - high.astype(np.float32)).astype(jnp.bfloat16)
    return jnp.asarray(high), jnp.asarray(low)


def inflow_of(leak):
    series = leak * (1.0 - leak * (0.5 - leak * (1.0 / 6.0 - leak * (1.0 / 24.0 - leak * (
        1.0 / 120.0 - leak * (1.0 / 720.0 - leak * (1.0 / 5040.0)))))))
    return jnp.where(leak < 0.5, series, 1.0 - jnp.exp(-leak))


def own_block_kernel(start_ref, pack_ref, coef_ref, msg_ref, loc_ref, wide):
    bands = coef_ref.shape[0]
    samples = msg_ref.shape[1]
    chans = pack_ref.shape[0]
    wide[...] = pack_ref[...].astype(jnp.float32).T
    lane = lax.broadcasted_iota(jnp.int32, (bands, chans), 1)
    leak = wide[samples : samples + bands, :]
    live = wide[samples + bands : samples + bands + 1, :]
    keep = jnp.exp(-leak)
    inflow = inflow_of(leak)
    coefs = [jnp.broadcast_to(coef_ref[:, i : i + 1], (bands, chans)) for i in range(5)]

    def ends(keep, inflow):
        after = keep
        total = keep
        step = 1
        while step < chans:
            rolled = pltpu.roll(after, chans - step, 1)
            after = after * jnp.where(lane < chans - step, rolled, 1.0)
            total = total * pltpu.roll(total, step, 1)
            step *= 2
        behind = jnp.where(lane < chans - 1, pltpu.roll(after, chans - 1, 1), 1.0)
        return behind * inflow, total

    offset = start_ref[0]
    weight_end, total_end = ends(keep, inflow)
    inside = lane < offset
    weight_loc, total_loc = ends(jnp.where(inside, keep, 1.0), jnp.where(inside, inflow, 0.0))
    msg_ref[...] = jnp.zeros_like(msg_ref)
    loc_ref[...] = jnp.zeros_like(loc_ref)
    zero = leak * 0.0
    tile = msg_ref[0:bands, :]
    time = lax.broadcasted_iota(jnp.int32, (bands, samples), 1)

    def step(t, state):
        x1, x2, y1, y2, end, loc = state
        x = jnp.broadcast_to(wide[pl.ds(t, 1), :], (bands, chans))
        y = coefs[0] * x + coefs[1] * x1 + coefs[2] * x2 - coefs[3] * y1 - coefs[4] * y2
        f = (live * y).astype(jnp.bfloat16).astype(jnp.float32)
        here = time == t
        end = jnp.where(here, jnp.sum(weight_end * f, axis=1, keepdims=True), end)
        loc = jnp.where(here, jnp.sum(weight_loc * f, axis=1, keepdims=True), loc)
        return x, x1, y, y1, end, loc

    state = lax.fori_loop(0, samples, step, (zero, zero, zero, zero, tile, tile), unroll=4)
    msg_ref[0:bands, :] = state[4]
    msg_ref[bands : 2 * bands, :] = total_end
    loc_ref[0:bands, :] = state[5]
    loc_ref[bands : 2 * bands, :] = total_loc


def exchange_kernel(count, near, pack_ref, msg_ref, packs_ref, msgs_ref, s1, r1, s2, r2):
    me = lax.axis_index("chan")
    barrier = pltpu.get_barrier_semaphore()
    for i in range(1, count):
        pl.semaphore_signal(
            barrier, inc=1, device_id={"chan": lax.rem(me + i, count)}, device_id_type=MESH
        )
    pl.semaphore_wait(barrier, count - 1)
    copies = []
    for i in range(1, count):
        copies.append(
            pltpu.make_async_remote_copy(
                src_ref=msg_ref,
                dst_ref=msgs_ref.at[me],
                send_sem=s1.at[i],
                recv_sem=r1.at[i],
                device_id={"chan": lax.rem(me + i, count)},
                device_id_type=MESH,
            )
        )
        copies[-1].start()
        if i <= near:
            copies.append(
                pltpu.make_async_remote_copy(
                    src_ref=pack_ref,
                    dst_ref=packs_ref.at[i - 1],
                    send_sem=s2.at[i],
                    recv_sem=r2.at[i],
                    device_id={"chan": lax.rem(me + count - i, count)},
                    device_id_type=MESH,
                )
            )
            copies[-1].start()
    for copy in copies:
        copy.wait()


def main_kernel(
    dims, info_ref, lists_ref, pack_ref, packs_ref, msgs_ref, loc_ref, coef_ref, delays_ref, hh_ref, hl_ref,
    out_ref, out2_ref, rows, wide, tabs, xt, energy, snap, delt, acc, acc2,
):
    samples, bands, chans, aperture, near, count = dims
    blocks = aperture // chans
    me = info_ref[1]
    offset = info_ref[0]
    points = samples * bands
    lead = (DMAX - 1) * bands

    rows[0:chans, :] = pack_ref[...].astype(jnp.float32)
    for j in range(near):
        inside = jnp.where(me + j + 1 < count, 1.0, 0.0)
        rows[(j + 1) * chans : (j + 2) * chans, :] = packs_ref[j].astype(jnp.float32) * inside
    span = (near + 1) * chans
    wide[...] = pltpu.roll(rows[...].T, span - offset, 1)[:, :aperture]
    delt[...] = delays_ref[...].T

    def add_device(i, state):
        return msgs_ref[i, bands : 2 * bands, 0:1] * state + msgs_ref[i, 0:bands, :]

    incoming = lax.fori_loop(0, me, add_device, jnp.zeros((bands, samples), jnp.float32))
    incoming = loc_ref[bands : 2 * bands, 0:1] * incoming + loc_ref[0:bands, :]

    lane = lax.broadcasted_iota(jnp.int32, (bands, chans), 1)
    steps = []
    size = 1
    while size < chans:
        steps.append(size)
        size *= 2
    for j in range(blocks):
        cols = slice(j * chans, (j + 1) * chans)
        leak = wide[samples : samples + bands, cols]
        prod = jnp.exp(-leak)
        for n, size in enumerate(steps):
            tabs[n * bands : (n + 1) * bands, cols] = jnp.where(lane >= size, prod, 0.0)
            prod = prod * jnp.where(lane >= size, pltpu.roll(prod, size, 1), 1.0)
        n = len(steps)
        tabs[n * bands : (n + 1) * bands, cols] = prod
        tabs[(n + 1) * bands : (n + 2) * bands, cols] = jnp.broadcast_to(
            prod[:, chans - 1 : chans], (bands, chans)
        )
        tabs[(n + 2) * bands : (n + 3) * bands, cols] = inflow_of(leak)
    live = wide[samples + bands : samples + bands + 1, :]
    xt[0:lead, :] = jnp.zeros((lead, aperture), jnp.bfloat16)
    energy[...] = jnp.zeros_like(energy)
    coefs = [jnp.broadcast_to(coef_ref[:, i : i + 1], (bands, chans)) for i in range(5)]
    time = lax.broadcasted_iota(jnp.int32, (bands, samples), 1)

    def tab(n, j):
        return tabs[n * bands : (n + 1) * bands, j * chans : (j + 1) * chans]

    def filter_step(t, state):
        x1, x2, y1s, y2s = state
        x = jnp.broadcast_to(wide[pl.ds(t, 1), :], (bands, aperture))
        carry = jnp.broadcast_to(
            jnp.sum(jnp.where(time == t, incoming, 0.0), axis=1, keepdims=True), (bands, chans)
        )
        slot = pl.multiple_of(jnp.maximum(t - (samples - DMAX), 0) * bands, bands)
        row = pl.multiple_of(lead + t * bands, bands)
        ys = []
        for j in range(blocks):
            cols = slice(j * chans, (j + 1) * chans)
            y = (
                coefs[0] * x[:, cols]
                + coefs[1] * x1[:, cols]
                + coefs[2] * x2[:, cols]
                - coefs[3] * y1s[j]
                - coefs[4] * y2s[j]
            )
            ys.append(y)
            f = (live[:, cols] * y).astype(jnp.bfloat16).astype(jnp.float32)
            v = tab(len(steps) + 2, j) * f
            for n, size in enumerate(steps):
                v = v + tab(n, j) * pltpu.roll(v, size, 1)
            mean = v + tab(len(steps), j) * carry
            if j + 1 < blocks:
                last = jnp.broadcast_to(v[:, chans - 1 : chans], (bands, chans))
                carry = last + tab(len(steps) + 1, j) * carry
            d = (live[:, cols] * (f - mean)).astype(jnp.bfloat16)
            xt[pl.ds(row, bands), cols] = d
            df = d.astype(jnp.float32)
            e = energy[:, cols] + df * df
            energy[:, cols] = e
            snap[pl.ds(slot, bands), cols] = e
        return x, x1, tuple(ys), y1s

    zero_row = energy[...]
    zeros = tuple(energy[:, j * chans : (j + 1) * chans] for j in range(blocks))
    lax.fori_loop(0, samples, filter_step, (zero_row, zero_row, zeros, zeros), unroll=2)

    tiles = delays_ref.shape[0] // LANES
    for j in range(tiles):
        acc[j] = jnp.zeros((points, LANES), jnp.float32)

    def add_delay(d, _):
        picked = jnp.where(delt[...] == d, 1.0, 0.0).astype(jnp.bfloat16)
        window = xt[pl.ds(pl.multiple_of((DMAX - 1 - d) * bands, bands), points), :]
        part = jnp.dot(window, picked, preferred_element_type=jnp.float32)
        for j in range(tiles):
            acc[j] += part[:, j * LANES : (j + 1) * LANES]
        return 0

    lax.fori_loop(0, DMAX, add_delay, 0)
    scale = 1.0 / math.sqrt(aperture)
    slow = delays_ref.shape[0]
    passes, slots = lists_ref.shape
    slow_id = lax.broadcasted_iota(jnp.int32, (1, slow), 1)
    nt_dims = (((1,), (1,)), ((), ()))
    pad = jnp.zeros((slots, DMAX * bands), jnp.float32)
    length = points + DMAX * bands
    norms = [
        jnp.sum(snap[(DMAX - d) * bands - bands : (DMAX - d) * bands, :], axis=0, keepdims=True)
        for d in range(DMAX)
    ]
    onehot = jnp.concatenate(
        [jnp.where(slow_id == lists_ref[0, r], 1.0, 0.0) for r in range(slots)], axis=0
    ).astype(jnp.bfloat16)
    guide = lax.dot_general(
        onehot,
        jnp.concatenate([(acc[j] * scale).astype(jnp.bfloat16) for j in range(tiles)], axis=1),
        nt_dims,
        preferred_element_type=jnp.float32,
    )
    results = []
    for i in range(passes):
        chosen = jnp.concatenate(
            [delays_ref[pl.ds(lists_ref[i, r], 1), :] for r in range(slots)], axis=0
        )
        guide = guide.astype(jnp.bfloat16).astype(jnp.float32)
        padded = jnp.concatenate([guide, pad], axis=1)
        shifted = [padded[:, :points]] + [
            pltpu.roll(padded, length - d * bands, 1)[:, :points] for d in range(1, DMAX)
        ]
        shifted = jnp.concatenate(shifted, axis=0).astype(jnp.bfloat16)
        products = jnp.dot(shifted, xt[lead : lead + points, :], preferred_element_type=jnp.float32)
        numerator = jnp.zeros((slots, aperture), jnp.float32)
        strength = jnp.zeros((slots, aperture), jnp.float32)
        for d in range(DMAX):
            match = chosen == d
            numerator = numerator + jnp.where(match, products[d * slots : (d + 1) * slots, :], 0.0)
            strength = strength + jnp.where(match, norms[d], 0.0)
        guide_norm = jnp.sqrt(jnp.sum(guide * guide, axis=1, keepdims=True) + EPS)
        coherence = numerator / (jnp.sqrt(strength + EPS) * guide_norm)
        weight = (live * (0.25 + jnp.maximum(coherence, 0.0))).astype(jnp.bfloat16).astype(jnp.float32)
        spread = jnp.concatenate(
            [jnp.where(chosen == d, weight, 0.0) for d in range(DMAX)], axis=0
        ).astype(jnp.bfloat16)
        parts = lax.dot_general(
            spread, xt[lead : lead + points, :], nt_dims, preferred_element_type=jnp.float32
        )
        refined = parts[0:slots, :]
        for d in range(1, DMAX):
            part = jnp.concatenate([parts[d * slots : (d + 1) * slots, :], pad], axis=1)
            refined = refined + pltpu.roll(part, d * bands, 1)[:, :points]
        refined = refined / jnp.sqrt(1.0 + jnp.sum(weight * weight, axis=1, keepdims=True))
        results.append(refined)
        guide = refined
    total = passes * slots
    results.append(jnp.zeros((LANES - total, points), jnp.float32))
    acc2[...] = jnp.concatenate(results, axis=0).T

    def envelope(band, _):
        s = jnp.concatenate(
            [acc.at[j][pl.ds(band, samples, stride=bands), :] * scale for j in range(tiles)]
            + [acc2[pl.ds(band, samples, stride=bands), :]],
            axis=1,
        )
        high = s.astype(jnp.bfloat16)
        low = (s - high.astype(jnp.float32)).astype(jnp.bfloat16)
        turned = (
            jnp.dot(hh_ref[...], high, preferred_element_type=jnp.float32)
            + jnp.dot(hh_ref[...], low, preferred_element_type=jnp.float32)
            + jnp.dot(hl_ref[...], high, preferred_element_type=jnp.float32)
        )
        power = (s * s + turned * turned).T.astype(jnp.bfloat16)
        cols = pl.ds(pl.multiple_of(band * samples, samples), samples)
        out_ref[:, cols] = power[:slow, :]
        out2_ref[:, cols] = power[slow : slow + total, :]
        return 0

    lax.fori_loop(0, bands, envelope, 0)


def per_device(traces, filter_coefs, leakage, live_mask, aperture_starts, delays, refine_lists):
    chans, samples = traces.shape
    bands = filter_coefs.shape[0]
    slow, aperture = delays.shape
    near = (aperture + chans - 1) // chans
    count = lax.axis_size("chan")
    me = lax.axis_index("chan").astype(jnp.int32)
    passes, slots = refine_lists.shape[1:]
    offset = aperture_starts[0] - me * chans
    info = jnp.stack([offset, me])
    width = -(-(samples + bands + 1) // LANES) * LANES
    pack = jnp.concatenate(
        [
            traces,
            leakage,
            live_mask.astype(jnp.bfloat16)[:, None],
            jnp.zeros((chans, width - samples - bands - 1), jnp.bfloat16),
        ],
        axis=1,
    )
    f32 = jnp.float32
    msg, loc = pl.pallas_call(
        own_block_kernel,
        out_shape=(
            jax.ShapeDtypeStruct((2 * bands, samples), f32),
            jax.ShapeDtypeStruct((2 * bands, samples), f32),
        ),
        in_specs=[SM, VM, VM],
        out_specs=(VM, VM),
        scratch_shapes=[pltpu.VMEM((width, chans), f32)],
    )(info, pack, filter_coefs)
    dma = pltpu.SemaphoreType.DMA
    packs, msgs = pl.pallas_call(
        functools.partial(exchange_kernel, count, near),
        out_shape=(
            jax.ShapeDtypeStruct((near, chans, width), jnp.bfloat16),
            jax.ShapeDtypeStruct((count, 2 * bands, samples), f32),
        ),
        in_specs=[HB, HB],
        out_specs=(HB, HB),
        scratch_shapes=[dma((count,)), dma((count,)), dma((near + 1,)), dma((near + 1,))],
        compiler_params=pltpu.CompilerParams(collective_id=0, has_side_effects=True),
    )(pack, msg)
    points = samples * bands
    hh, hl = hilbert_parts(samples)
    levels = (chans - 1).bit_length() + 3
    beam, refined = pl.pallas_call(
        functools.partial(main_kernel, (samples, bands, chans, aperture, near, count)),
        out_shape=(
            jax.ShapeDtypeStruct((slow, bands * samples), jnp.bfloat16),
            jax.ShapeDtypeStruct((passes * slots, bands * samples), jnp.bfloat16),
        ),
        in_specs=[SM, SM] + [VM] * 8,
        out_specs=(VM, VM),
        scratch_shapes=[
            pltpu.VMEM(((near + 1) * chans, width), f32),
            pltpu.VMEM((width, aperture), f32),
            pltpu.VMEM((levels * bands, aperture), f32),
            pltpu.VMEM((points + (DMAX - 1) * bands, aperture), jnp.bfloat16),
            pltpu.VMEM((bands, aperture), f32),
            pltpu.VMEM((DMAX * bands, aperture), f32),
            pltpu.VMEM((aperture, slow), jnp.int32),
            pltpu.VMEM((slow // LANES, points, LANES), f32),
            pltpu.VMEM((points, LANES), f32),
        ],
        compiler_params=pltpu.CompilerParams(vmem_limit_bytes=48 * 1024 * 1024),
    )(info, refine_lists[0], pack, packs, msgs, loc, filter_coefs, delays, hh, hl)
    return (
        beam.reshape(1, slow, bands, samples),
        refined.reshape(1, passes, slots, bands, samples),
    )


def solution(mesh):
    return jax.shard_map(
        per_device,
        mesh=mesh,
        in_specs=(
            P(("cables", "chan"), None),
            P(),
            P(("cables", "chan"), None),
            P(("cables", "chan")),
            P(("cables", "chan")),
            P(),
            P(("cables", "chan"), None, None),
        ),
        out_specs=(
            P(("cables", "chan"), None, None, None),
            P(("cables", "chan"), None, None, None, None),
        ),
        check_vma=False,
    )
```

time: 603 us -> 97.2 us (0.16)
  local copies, waits for them, and re-layouts: 217 us -> 8.26 us
  other arithmetic: 154 us -> 1.37 us
  matrix products: 118 us -> 0 us
  Pallas kernels: 0 us -> 85.7 us
  waiting for transfers between devices: 48 us -> 0 us
  blocking collectives: 40.9 us -> 0 us
  starting transfers between devices: 10.5 us -> 0 us
    dynamic_slice x113 -> x0, local copies, waits for them, and re-layouts: 136 us -> none  [the longest x48 93.7 us: shifted_window(): section = lax.dynamic_index_in_dim(copies, delay_now, 0, keepdims=False)]
    dot_general x88 -> x0, matrix products: 118 us -> none  [the longest x16 58.3 us: add_delay(): jnp.dot(picked, shifted_window(copies, delay_now), preferred_element_type...]
    reduce_sum x35 -> x0, other arithmetic: 91.8 us -> none  [the longest x32 91.2 us: measure(): squares = jnp.sum(jnp.square(window.astype(jnp.float32)), axis=1)]
    pallas_call x0 -> x3, Pallas kernels: none -> 85.7 us  [the longest x1 62.6 us: per_device(): pl.pallas_call(functools.partial(main_kernel, (samples, bands, chans, ape...]
    ppermute x8 -> x0, waiting for transfers between devices: 48 us -> none  [passed_along(): return lax.ppermute(block, axis, route)]
    unnamed x34 -> x32, local copies, waits for them, and re-layouts: 54.4 us -> 8.05 us
    convert_element_type x69 -> x0, other arithmetic: 44.6 us -> none  [the longest x68 44 us: unit_vector(): (positions == place).astype(jnp.float32)[None]]
    all_gather x2 -> x0, blocking collectives: 40.9 us -> none  [prefix(): gathered = jax.tree.map(lambda a: lax.all_gather(a, axis), part)]
  transfers between devices with their start and end apart: 8 -> 0, of which waited for: 4 -> 0; matrix products, arithmetic and copies ran while one was open for 1% -> 0% of each run, Pallas kernels for 0% -> 0%
where the time goes in v1:
time: 97.2 us; the launch traced here: 96.7 us
  Pallas kernels  85.7 us (88%)
  local copies, waits for them, and re-layouts  8.26 us (8%)
  between operations  1.38 us (1%)
  other arithmetic  1.37 us (1%)
    pallas_call x1, Pallas kernels, per_device(): pl.pallas_call(functools.partial(main_kernel, (samples, bands, chans, ape...  62.6 us
    pallas_call x1, Pallas kernels, per_device(): pl.pallas_call(functools.partial(exchange_kernel, count, near), out_shape...  17.7 us
    unnamed x32, local copies, waits for them, and re-layouts  8.05 us
    pallas_call x1, Pallas kernels, per_device(): pl.pallas_call(own_block_kernel, out_shape=(jax.ShapeDtypeStruct((2 * ban...  5.43 us

profile of v1, /device:TPU:0, one launch (start us, length us, event | category | flops | bytes accessed | tf_op | source)
XLA Modules:
  0.0 96.7 jit_solution(15391851847491297336)
XLA Ops:
  1.3 0.0 copy-start.13
  1.3 0.6 pad_add_fusion.start_ref.info_ref
  1.9 0.0 copy-start.11
  1.9 0.0 copy-done.13
  2.0 0.1 pad.3.clone
  2.0 0.6 copy-done.11
  2.6 0.0 copy-start.12
  2.6 0.7 copy.13.coef_ref
  3.3 0.0 copy-start.10
  3.3 0.1 copy.12
  3.4 0.0 copy-done.12
  3.4 0.1 copy.11
  3.6 0.5 copy-done.10
  4.1 0.7 maximum_maximum_fusion.pack_ref
  4.8 0.0 copy-start
  4.8 5.4 %shard_map.104 = (f32[32,128]{1,0:T(8,128)}, f32[32,128]{1,0:T(8,128)}) custom-call(s32[2]{0:T(128)} %pad_add_fusion.start_ref.info_ref, bf16[128,256]{1,0:T(8,128)(2,1)} %maximum_maximum_fusion.pack_ref, f32[16,5]{1,0:T(8,128)} %copy.13.coef_ref), custom_call_target="tpu_custom_call" | custom-call | tf_op jit(solution)/shard_map/pallas_call | solution.py:334
  10.2 17.7 %shard_map.105 = (bf16[4,128,256]{2,1,0:T(8,128)(2,1)}, f32[16,32,128]{2,1,0:T(8,128)}) custom-call(bf16[128,256]{1,0:T(8,128)(2,1)} %maximum_maximum_fusion.pack_ref, f32[32,128]{1,0:T(8,128)} %get-tuple-element.8.msg_ref), custom_call_target="tpu_custom_call" | custom-call | tf_op jit(solution)/shard_map/pallas_call | solution.py:345
  27.9 0.0 copy-start.8
  28.0 0.0 copy-start.9
  28.0 0.0 copy-done
  28.0 0.0 copy-done.4
  28.0 0.0 copy-done.5
  28.0 0.0 copy-done.6
  28.0 0.6 copy-done.8
  28.6 0.0 copy-done.9
  28.6 1.0 %copy-done.1 = s32[256,512]{1,0:T(8,128)S(1)} copy-done((s32[256,512]{1,0:T(8,128)S(1)}, s32[256,512]{1,0:T(8,128)}, u32[]{:S(2)}) %copy-start.1) | copy-done | bytes 524312
  29.7 0.9 copy-done.2
  30.6 0.9 copy-done.3
  31.6 0.7 copy-done.7
  32.3 62.6 %shard_map.106 = (bf16[256,2048]{1,0:T(8,128)(2,1)S(1)}, bf16[16,2048]{1,0:T(8,128)(2,1)S(1)}) custom-call(s32[2]{0:T(128)S(1)} %copy-done.8, s32[2,8]{1,0:T(2,128)S(1)} %bitcast.13, bf16[128,256]{1,0:T(8,128)(2,1)S(1)} %copy-done, bf16[4,128,256]{2,1,0:T(8,128)(2,1)S(1)} %copy-done.2, f32[16,32,128]{2,1,0:T(8,128)S(1)} %copy-done.3, ...), custom_call_target="tpu_custom_call" | custom-call | tf_op jit(solution)/shard_map/pallas_call | solution.py:359
  94.9 1.2 %copy.16 = bf16[32,8,16,128]{3,2,1,0:T(8,128)(2,1)} copy(bf16[32,8,16,128]{3,1,2,0:T(8,128)(2,1)S(1)} %bitcast.11) | data formatting | bytes 2097152
  96.1 0.6 copy.15
  (9 shorter events, 0.0 us)
Async XLA Ops:
  1.3 0.7 copy-start.13
  1.9 0.7 copy-start.11
  2.6 0.8 copy-start.12
  3.3 0.8 copy-start.10
  4.8 23.2 %copy-start = (bf16[128,256]{1,0:T(8,128)(2,1)S(1)}, bf16[128,256]{1,0:T(8,128)(2,1)}, u32[]{:S(2)}) copy-start(bf16[128,256]{1,0:T(8,128)(2,1)} %maximum_maximum_fusion.pack_ref) | copy-start | bytes 196612
  10.2 17.8 %copy-start.4 = (f32[16,5]{1,0:T(8,128)S(1)}, f32[16,5]{1,0:T(8,128)}, u32[]{:S(2)}) copy-start(f32[16,5]{1,0:T(8,128)} %copy.13.coef_ref) | copy-start | bytes 964
  10.2 17.8 %copy-start.5 = (bf16[128,128]{1,0:T(8,128)(2,1)S(1)}, bf16[128,128]{1,0:T(8,128)(2,1)}, u32[]{:S(2)}) copy-start(bf16[128,128]{1,0:T(8,128)(2,1)} %constant.13.clone.hl_ref) | copy-start | bytes 98308
  10.2 17.8 %copy-start.6 = (bf16[128,128]{1,0:T(8,128)(2,1)S(1)}, bf16[128,128]{1,0:T(8,128)(2,1)}, u32[]{:S(2)}) copy-start(bf16[128,128]{1,0:T(8,128)(2,1)} %constant.12.clone.hh_ref) | copy-start | bytes 98308
  27.9 0.7 copy-start.8
  28.0 0.7 copy-start.9
  28.6 1.0 %copy-start.1 = (s32[256,512]{1,0:T(8,128)S(1)}, s32[256,512]{1,0:T(8,128)}, u32[]{:S(2)}) copy-start(s32[256,512]{1,0:T(8,128)} %delays_ref.1) | copy-start | bytes 1572868
  29.7 0.9 copy-start.2
  30.6 0.9 copy-start.3
  31.6 0.7 copy-start.7
